TPU v7x, 32 devices: a whole 2x2x4 slice. The times are simulated.
32 devices in a mesh: fsdp: 8 (over z, x), seq: 4 (over y, core).
Axes of the slice: x: 2, y: 2, z: 4, core: 2. Of those that a mesh axis runs over, the one named last changes fastest.
Arguments:
- tokens: bfloat16 [16384, 768], P(('fsdp', 'seq')), may hold values from -6 to 6
- read_memory: bfloat16 [8, 10, 768], P('fsdp'), may hold values from -6 to 6
- write_memory: bfloat16 [8, 10, 768], P('fsdp'), may hold values from -6 to 6
- lengths: int32 [8], P('fsdp'), may hold values from 1024 to 2048, as said below
- qkv_weight: bfloat16 [768, 2304], P('fsdp'), may hold values from -0.21875 to 0.21875
- qv_bias: bfloat16 [1536], P('fsdp'), may hold values from -1.5 to 1.5
- out_weight: bfloat16 [768, 768], P('fsdp'), may hold values from -6 to 6
- out_bias: bfloat16 [768], P('fsdp'), may hold values from -1.5 to 1.5
- norm1_gain: bfloat16 [768], P('fsdp'), may hold values from 0.5 to 1.5
- norm1_bias: bfloat16 [768], P('fsdp'), may hold values from -1.5 to 1.5
- up_weight: bfloat16 [768, 3072], P('fsdp'), may hold values from -0.21875 to 0.21875
- up_bias: bfloat16 [3072], P('fsdp'), may hold values from -1.5 to 1.5
- down_weight: bfloat16 [3072, 768], P('fsdp'), may hold values from -0.109375 to 0.109375
- down_bias: bfloat16 [768], P('fsdp'), may hold values from -1.5 to 1.5
- norm2_gain: bfloat16 [768], P('fsdp'), may hold values from 0.5 to 1.5
- norm2_bias: bfloat16 [768], P('fsdp'), may hold values from -1.5 to 1.5
- cotangent: bfloat16 [16384, 768], P(('fsdp', 'seq')), may hold values from -6 to 6
Outputs:
- output: bfloat16 [16384, 768], P(('fsdp', 'seq'))
- input_grad: float32 [16384, 768], P(('fsdp', 'seq'))
- read_grad: float32 [8, 10, 768], P('fsdp')
- write_grad: float32 [8, 10, 768], P('fsdp')
- qkv_weight_grad: float32 [768, 2304], P('fsdp')
- qv_bias_grad: float32 [1536], P('fsdp')
- out_weight_grad: float32 [768, 768], P('fsdp')
- out_bias_grad: float32 [768], P('fsdp')
- norm1_gain_grad: float32 [768], P('fsdp')
- norm1_bias_grad: float32 [768], P('fsdp')
- up_weight_grad: float32 [768, 3072], P('fsdp')
- up_bias_grad: float32 [3072], P('fsdp')
- down_weight_grad: float32 [3072, 768], P('fsdp')
- down_bias_grad: float32 [768], P('fsdp')
- norm2_gain_grad: float32 [768], P('fsdp')
- norm2_bias_grad: float32 [768], P('fsdp')
Inputs may be any that keep to these rules, and one draw needn't show every extreme that they name: `lengths`: valid length of each slot in positions, counting its 10 read and 10 write memory tokens; in every draw some slot has length 2048 and some slot 1024.
All inputs are finite; a program needn't handle non-finite values.
Results may differ from a plain program's by a relative error of at most 0.017.
Values may be sent and summed in bfloat16 or wider, within the bound.
A program may use at most 128 MiB of HBM per device.

v0:
```python
from functools import partial
import jax
import jax.numpy as jnp
from jax import lax
from jax.sharding import PartitionSpec as P

HEAD = 64
MEM = 10
norm_epsilon = 1e-06
masked_score = -1e30


def normalize(values, gain_vec, shift_vec):
    centre = values - jnp.mean(values, axis=-1, keepdims=True)
    factor = lax.rsqrt(jnp.mean(centre * centre, axis=-1, keepdims=True) + norm_epsilon)
    return centre * factor * gain_vec + shift_vec


def over_rows(left, right):
    return lax.dot_general(
        left, right, (((0,), (0,)), ((), ())), preferred_element_type=jnp.float32
    )


def by_columns(left, right):
    return lax.dot_general(
        left, right, (((1,), (1,)), ((), ())), preferred_element_type=jnp.float32
    )


def column_sums(values):
    return jnp.sum(values, axis=0, dtype=jnp.float32)


def per_device(
    tokens,
    read_memory,
    write_memory,
    lengths,
    qkv_weight,
    qv_bias,
    out_weight,
    out_bias,
    norm1_gain,
    norm1_bias,
    up_weight,
    up_bias,
    down_weight,
    down_bias,
    norm2_gain,
    norm2_bias,
    cotangent,
):
    seq_count = lax.axis_size("seq")
    local_rows = tokens.shape[0]
    model_width = tokens.shape[1]
    slot_rows = local_rows * seq_count
    head_cols = model_width // seq_count
    head_count = head_cols // HEAD
    block_rows = min(512, slot_rows)
    block_count = slot_rows // block_rows
    factor = HEAD ** (-0.5)
    length = lengths[0]
    places = lax.axis_index("seq") * local_rows + jnp.arange(local_rows, dtype=jnp.int32)
    in_slot = (places < length)[:, None]
    memory_slots = jnp.arange(MEM, dtype=jnp.int32)
    pick_read = places[:, None] == memory_slots[None, :]
    pick_write = places[:, None] == length - MEM + memory_slots[None, :]
    is_memory = jnp.any(pick_read | pick_write, axis=1)[:, None]
    read_float = pick_read.astype(jnp.float32)
    write_float = pick_write.astype(jnp.float32)
    memory_rows = jnp.dot(
        read_float.astype(jnp.bfloat16), read_memory[0], preferred_element_type=jnp.float32
    ) + jnp.dot(
        write_float.astype(jnp.bfloat16), write_memory[0], preferred_element_type=jnp.float32
    )
    layer_in = jnp.where(is_memory, memory_rows.astype(jnp.bfloat16), tokens)
    qkv_full, qv_full, out_full, out_bias_full, gain_one, shift_one = (
        lax.all_gather(qkv_weight, "fsdp", axis=0, tiled=True),
        lax.all_gather(qv_bias, "fsdp", axis=0, tiled=True),
        lax.all_gather(out_weight, "fsdp", axis=0, tiled=True),
        lax.all_gather(out_bias, "fsdp", axis=0, tiled=True),
        lax.all_gather(norm1_gain, "fsdp", axis=0, tiled=True),
        lax.all_gather(norm1_bias, "fsdp", axis=0, tiled=True),
    )
    projected = jnp.dot(layer_in, qkv_full, preferred_element_type=jnp.float32)
    qv_vec = qv_full.astype(jnp.float32)
    query_tok = (projected[:, :model_width] + qv_vec[:model_width]).astype(jnp.bfloat16)
    keys_tok = projected[:, model_width : 2 * model_width].astype(jnp.bfloat16)
    values_tok = (projected[:, 2 * model_width :] + qv_vec[model_width:]).astype(jnp.bfloat16)
    heads_query, heads_key, heads_value = (
        lax.all_to_all(query_tok, "seq", split_axis=1, concat_axis=0, tiled=True),
        lax.all_to_all(keys_tok, "seq", split_axis=1, concat_axis=0, tiled=True),
        lax.all_to_all(values_tok, "seq", split_axis=1, concat_axis=0, tiled=True),
    )
    heads_query = heads_query.reshape(slot_rows, head_count, HEAD)
    heads_key = heads_key.reshape(slot_rows, head_count, HEAD)
    heads_value = heads_value.reshape(slot_rows, head_count, HEAD)
    key_in_slot = jnp.arange(slot_rows, dtype=jnp.int32) < length

    def scores_for(query_block):
        scores = (
            jnp.einsum("qhd,khd->hqk", query_block, heads_key, preferred_element_type=jnp.float32)
            * factor
        )
        return jnp.where(key_in_slot[None, None, :], scores, masked_score)

    def forward_block(block_index):
        query_block = lax.dynamic_slice_in_dim(heads_query, block_index * block_rows, block_rows, 0)
        scores = scores_for(query_block)
        row_max = jnp.max(scores, axis=-1, keepdims=True)
        exponent = jnp.exp(scores - row_max)
        row_sum = jnp.sum(exponent, axis=-1, keepdims=True)
        probs_low = (exponent / row_sum).astype(jnp.bfloat16)
        mixed_block = jnp.einsum(
            "hqk,khd->qhd", probs_low, heads_value, preferred_element_type=jnp.float32
        )
        return (mixed_block.astype(jnp.bfloat16), row_max, row_sum)

    mixed_blocks, row_maxes, row_sums = lax.map(
        forward_block, jnp.arange(block_count, dtype=jnp.int32)
    )
    mixed_heads = mixed_blocks.reshape(slot_rows, head_cols)
    attended = lax.all_to_all(mixed_heads, "seq", split_axis=0, concat_axis=1, tiled=True)
    branch = jnp.dot(attended, out_full, preferred_element_type=jnp.float32) + out_bias_full.astype(
        jnp.float32
    )
    resid_one = layer_in.astype(jnp.float32) + branch
    middle, norm_one_back = jax.vjp(
        normalize, resid_one, gain_one.astype(jnp.float32), shift_one.astype(jnp.float32)
    )
    up_full, up_bias_full, down_full, down_bias_full, gain_two, shift_two = (
        lax.all_gather(up_weight, "fsdp", axis=0, tiled=True),
        lax.all_gather(up_bias, "fsdp", axis=0, tiled=True),
        lax.all_gather(down_weight, "fsdp", axis=0, tiled=True),
        lax.all_gather(down_bias, "fsdp", axis=0, tiled=True),
        lax.all_gather(norm2_gain, "fsdp", axis=0, tiled=True),
        lax.all_gather(norm2_bias, "fsdp", axis=0, tiled=True),
    )
    middle_low = middle.astype(jnp.bfloat16)
    up_pre = jnp.dot(middle_low, up_full, preferred_element_type=jnp.float32) + up_bias_full.astype(
        jnp.float32
    )
    gelu_out, gelu_back = jax.vjp(partial(jax.nn.gelu, approximate=False), up_pre)
    hidden = gelu_out.astype(jnp.bfloat16)
    down_pre = jnp.dot(
        hidden, down_full, preferred_element_type=jnp.float32
    ) + down_bias_full.astype(jnp.float32)
    final, norm_two_back = jax.vjp(
        normalize, middle + down_pre, gain_two.astype(jnp.float32), shift_two.astype(jnp.float32)
    )
    output = jnp.where(in_slot, final, 0.0).astype(jnp.bfloat16)
    grad_final = jnp.where(in_slot, cotangent.astype(jnp.float32), 0.0)
    down_back, up_back = (
        lax.all_gather(down_weight, "fsdp", axis=0, tiled=True),
        lax.all_gather(up_weight, "fsdp", axis=0, tiled=True),
    )
    grad_resid_two, grad_gain_two, grad_shift_two = norm_two_back(grad_final)
    grad_down = grad_resid_two.astype(jnp.bfloat16)
    grad_down_bias = column_sums(grad_down)
    grad_down_weight = over_rows(hidden, grad_down)
    grad_hidden = by_columns(grad_down, down_back)
    (grad_up_pre,) = gelu_back(grad_hidden)
    grad_up = grad_up_pre.astype(jnp.bfloat16)
    grad_up_bias = column_sums(grad_up)
    grad_up_weight = over_rows(middle_low, grad_up)
    grad_middle = grad_resid_two + by_columns(grad_up, up_back)
    grad_resid_one, grad_gain_one, grad_shift_one = norm_one_back(grad_middle)
    out_back, qkv_back = (
        lax.all_gather(out_weight, "fsdp", axis=0, tiled=True),
        lax.all_gather(qkv_weight, "fsdp", axis=0, tiled=True),
    )
    grad_branch = grad_resid_one.astype(jnp.bfloat16)
    grad_out_bias = column_sums(grad_branch)
    grad_out_weight = over_rows(attended, grad_branch)
    grad_attended = by_columns(grad_branch, out_back).astype(jnp.bfloat16)
    grad_heads = lax.all_to_all(grad_attended, "seq", split_axis=1, concat_axis=0, tiled=True)
    grad_heads = grad_heads.reshape(slot_rows, head_count, HEAD)

    def backward_block(carry, block_item):
        key_sum, value_sum = carry
        block_index, row_max, row_sum = block_item
        query_block = lax.dynamic_slice_in_dim(heads_query, block_index * block_rows, block_rows, 0)
        grad_block = lax.dynamic_slice_in_dim(grad_heads, block_index * block_rows, block_rows, 0)
        scores = scores_for(query_block)
        attn_probs = jnp.exp(scores - row_max) / row_sum
        probs_low = attn_probs.astype(jnp.bfloat16)
        grad_probs = jnp.einsum(
            "qhd,khd->hqk", grad_block, heads_value, preferred_element_type=jnp.float32
        )
        row_delta = jnp.sum(grad_probs * attn_probs, axis=-1, keepdims=True)
        grad_scores = (attn_probs * (grad_probs - row_delta)).astype(jnp.bfloat16)
        grad_query = (
            jnp.einsum("hqk,khd->qhd", grad_scores, heads_key, preferred_element_type=jnp.float32)
            * factor
        )
        key_sum = (
            key_sum
            + jnp.einsum(
                "hqk,qhd->khd", grad_scores, query_block, preferred_element_type=jnp.float32
            )
            * factor
        )
        value_sum = value_sum + jnp.einsum(
            "hqk,qhd->khd", probs_low, grad_block, preferred_element_type=jnp.float32
        )
        return ((key_sum, value_sum), grad_query.astype(jnp.bfloat16))

    zero_heads = jnp.zeros((slot_rows, head_count, HEAD), jnp.float32)
    (key_total, value_total), query_blocks = lax.scan(
        backward_block,
        (zero_heads, zero_heads),
        (jnp.arange(block_count, dtype=jnp.int32), row_maxes, row_sums),
    )
    grad_query_heads = query_blocks.reshape(slot_rows, head_cols)
    grad_key_heads = key_total.reshape(slot_rows, head_cols).astype(jnp.bfloat16)
    grad_value_heads = value_total.reshape(slot_rows, head_cols).astype(jnp.bfloat16)
    grad_query_tok, grad_key_tok, grad_value_tok = (
        lax.all_to_all(grad_query_heads, "seq", split_axis=0, concat_axis=1, tiled=True),
        lax.all_to_all(grad_key_heads, "seq", split_axis=0, concat_axis=1, tiled=True),
        lax.all_to_all(grad_value_heads, "seq", split_axis=0, concat_axis=1, tiled=True),
    )
    grad_projected = jnp.concatenate([grad_query_tok, grad_key_tok, grad_value_tok], axis=1)
    grad_qv_bias = jnp.concatenate([column_sums(grad_query_tok), column_sums(grad_value_tok)])
    grad_qkv_weight = over_rows(layer_in, grad_projected)
    grad_layer_in = grad_resid_one + by_columns(grad_projected, qkv_back)
    input_grad = jnp.where(is_memory, 0.0, grad_layer_in)
    grad_read = lax.dot_general(
        read_float,
        grad_layer_in,
        (((0,), (0,)), ((), ())),
        precision=lax.Precision.HIGHEST,
        preferred_element_type=jnp.float32,
    )
    grad_write = lax.dot_general(
        write_float,
        grad_layer_in,
        (((0,), (0,)), ((), ())),
        precision=lax.Precision.HIGHEST,
        preferred_element_type=jnp.float32,
    )
    (
        shard_qkv,
        shard_qv,
        shard_out_w,
        shard_out_b,
        shard_gain_one,
        shard_shift_one,
        shard_up_w,
        shard_up_b,
        shard_down_w,
        shard_down_b,
        shard_gain_two,
        shard_shift_two,
    ) = (
        lax.psum_scatter(grad_qkv_weight, "fsdp", scatter_dimension=0, tiled=True),
        lax.psum_scatter(grad_qv_bias, "fsdp", scatter_dimension=0, tiled=True),
        lax.psum_scatter(grad_out_weight, "fsdp", scatter_dimension=0, tiled=True),
        lax.psum_scatter(grad_out_bias, "fsdp", scatter_dimension=0, tiled=True),
        lax.psum_scatter(grad_gain_one, "fsdp", scatter_dimension=0, tiled=True),
        lax.psum_scatter(grad_shift_one, "fsdp", scatter_dimension=0, tiled=True),
        lax.psum_scatter(grad_up_weight, "fsdp", scatter_dimension=0, tiled=True),
        lax.psum_scatter(grad_up_bias, "fsdp", scatter_dimension=0, tiled=True),
        lax.psum_scatter(grad_down_weight, "fsdp", scatter_dimension=0, tiled=True),
        lax.psum_scatter(grad_down_bias, "fsdp", scatter_dimension=0, tiled=True),
        lax.psum_scatter(grad_gain_two, "fsdp", scatter_dimension=0, tiled=True),
        lax.psum_scatter(grad_shift_two, "fsdp", scatter_dimension=0, tiled=True),
    )
    (
        sum_qkv,
        sum_qv,
        sum_out_w,
        sum_out_b,
        sum_gain_one,
        sum_shift_one,
        sum_up_w,
        sum_up_b,
        sum_down_w,
        sum_down_b,
        sum_gain_two,
        sum_shift_two,
        read_total,
        write_total,
    ) = (
        lax.psum(shard_qkv.astype(jnp.bfloat16), "seq").astype(jnp.float32),
        lax.psum(shard_qv.astype(jnp.bfloat16), "seq").astype(jnp.float32),
        lax.psum(shard_out_w.astype(jnp.bfloat16), "seq").astype(jnp.float32),
        lax.psum(shard_out_b.astype(jnp.bfloat16), "seq").astype(jnp.float32),
        lax.psum(shard_gain_one.astype(jnp.bfloat16), "seq").astype(jnp.float32),
        lax.psum(shard_shift_one.astype(jnp.bfloat16), "seq").astype(jnp.float32),
        lax.psum(shard_up_w.astype(jnp.bfloat16), "seq").astype(jnp.float32),
        lax.psum(shard_up_b.astype(jnp.bfloat16), "seq").astype(jnp.float32),
        lax.psum(shard_down_w.astype(jnp.bfloat16), "seq").astype(jnp.float32),
        lax.psum(shard_down_b.astype(jnp.bfloat16), "seq").astype(jnp.float32),
        lax.psum(shard_gain_two.astype(jnp.bfloat16), "seq").astype(jnp.float32),
        lax.psum(shard_shift_two.astype(jnp.bfloat16), "seq").astype(jnp.float32),
        lax.psum(grad_read.astype(jnp.bfloat16), "seq").astype(jnp.float32),
        lax.psum(grad_write.astype(jnp.bfloat16), "seq").astype(jnp.float32),
    )
    return (
        output,
        input_grad,
        read_total[None],
        write_total[None],
        sum_qkv,
        sum_qv,
        sum_out_w,
        sum_out_b,
        sum_gain_one,
        sum_shift_one,
        sum_up_w,
        sum_up_b,
        sum_down_w,
        sum_down_b,
        sum_gain_two,
        sum_shift_two,
    )


def solution(mesh):
    in_specs = (
        P(("fsdp", "seq"), None),
        P("fsdp", None, None),
        P("fsdp", None, None),
        P("fsdp"),
        P("fsdp", None),
        P("fsdp"),
        P("fsdp", None),
        P("fsdp"),
        P("fsdp"),
        P("fsdp"),
        P("fsdp", None),
        P("fsdp"),
        P("fsdp", None),
        P("fsdp"),
        P("fsdp"),
        P("fsdp"),
        P(("fsdp", "seq"), None),
    )
    out_specs = (
        P(("fsdp", "seq"), None),
        P(("fsdp", "seq"), None),
        P("fsdp", None, None),
        P("fsdp", None, None),
        P("fsdp", None),
        P("fsdp"),
        P("fsdp", None),
        P("fsdp"),
        P("fsdp"),
        P("fsdp"),
        P("fsdp", None),
        P("fsdp"),
        P("fsdp", None),
        P("fsdp"),
        P("fsdp"),
        P("fsdp"),
    )
    return jax.shard_map(
        per_device, mesh=mesh, in_specs=in_specs, out_specs=out_specs, check_vma=False
    )
```

profile of v0, /device:TPU:0, one launch (start us, length us, event | category | flops | bytes accessed | tf_op | source)
XLA Modules:
  0.0 1022.8 jit_solution(4488948586990560364)
XLA Ops:
  18.6 39.7 %all-reduce.16 = (bf16[1536]{0:T(1024)(128)(2,1)S(1)}, bf16[768]{0:T(1024)(128)(2,1)S(1)}, bf16[768]{0:T(1024)(128)(2,1)S(1)}, bf16[768]{0:T(1024)(128)(2,1)S(1)...) all-reduce(bf16[1536]{0:T(1024)(128)(2,1)S(1)} %dynamic-update-slic, ...), channel_id=1, replica_groups=mesh['fsdp'=8,'seq'=4] {'fsdp'}, use_global_device_ids=true, to_apply=%add | all-reduce | flops 6144 | bytes 24576
  60.5 18.2 %all-gather.6.cloned.1.call-done = bf16[768,2304]{1,0:T(8,128)(2,1)} async-done(((bf16[96,2304]{1,0:T(8,128)(2,1)}), bf16[768,2304]{1,0:T(8,128)(2,1)}) %all-gather.6.cloned.1.call-update) | async-done | bytes 3538960 | tf_op jit(solution)/shard_map/all_gather | solution.py:79
  78.8 4.0 fusion.80
  91.0 10.5 %all-to-all-done = bf16[512,4,192]{0,2,1:T(8,128)(2,1)S(1)} async-done(((bf16[512,4,192]{0,2,1:T(8,128)(2,1)}), bf16[512,4,192]{0,2,1:T(8,128)(2,1)S(1)}, u32[]{:S(2)}, u32[]{:S(2)}) %all-to-all-start) | async-done | bytes 786464 | tf_op jit(solution)/shard_map/all_to_all | solution.py:92
  107.7 9.0 all-to-all-done.2
  125.5 6.2 all-to-all-done.1
  136.3 44.2 %while.30 = (s32[]{:T(128)}, bf16[4,512,3,64]{1,3,2,0:T(8,128)(2,1)}, f32[4,3,512,1]{2,1,3,0:T(4,128)S(1)}, f32[4,3,512,1]{2,1,3,0:T(4,128)S(1)}, s32[4]{0:T(128...) while((s32[]{:T(128)}, ...), condition=%wide.region_4.5_spmd.clone, body=%wide.region_1.4_spmd.clone.sunk | while | flops 843152384 | bytes 39787204 | solution.py:120
  143.0 4.3 fusion.133
  154.1 4.3 fusion.133
  165.1 4.3 fusion.133
  176.2 4.3 fusion.133
  184.1 26.3 %all-gather = bf16[8,1,384]{2,1,0:T(2,128)(2,1)S(1)} all-gather(bf16[1,1,384]{2,1,0:T(2,128)(2,1)S(1)} %reshape.204), channel_id=1, replica_groups=mesh['fsdp'=8,'seq'=4] {'fsdp'}, dimensions={0}, use_global_device_ids=true | all-gather | bytes 6912 | tf_op jit(solution)/shard_map/all_gather | solution.py:134
  214.5 20.9 %multiply_convert_fusion.1 = (bf16[512,3072]{1,0:T(8,128)(2,1)}, f32[512,3072]{1,0:T(8,128)}, f32[512,3072]{1,0:T(8,128)}) fusion(f32[3072]{0:T(1024)S(1)} %bitcast.154, bf16[768,3072]{1,0:T(8,128)(2,1)} %all-gather.10.cloned.1.call-done, f32[512,768]{1,0:T(8,128)} %copy-done.7, f32[768]{0:T(1024)S(1)} %convert_element_type.216, ...), kind=kOutput, calls=%fused_computation.49 | convolution fusion | flops 2521694208 | bytes 22042624 | tf_op jit(solution)/shard_map/dot_general | solution.py:141
  235.4 46.2 %all-gather.12.cloned.1.call-done = bf16[3072,768]{1,0:T(8,128)(2,1)} async-done(((bf16[384,768]{1,0:T(8,128)(2,1)}), bf16[3072,768]{1,0:T(8,128)(2,1)}) %all-gather.12.cloned.1.call-update) | async-done | bytes 4718608 | tf_op jit(solution)/shard_map/all_gather | solution.py:135
  281.6 6.1 fusion.79
  292.0 8.9 convert_reduce_fusion
  300.9 3.6 multiply_reduce_fusion.2
  309.1 4.2 all-to-all-start.4
  316.8 8.2 all-to-all-done.4
  331.4 115.4 %while.31 = (s32[]{:T(128)}, f32[2048,3,64]{0,2,1:T(8,128)S(1)}, f32[2048,3,64]{0,2,1:T(8,128)}, bf16[4,512,3,64]{1,3,2,0:T(8,128)(2,1)}, s32[4]{0:T(128)S(1)}, ...) while((s32[]{:T(128)}, f32[2048,3,64]{0,2,1:T(8,128)S(1)}, ...), condition=%wide.region_15.16_spmd.clone, body=%wide.region_13.15_spmd.clone.sunk | while | flops 2046886400 | bytes 204722992 | solution.py:210
  333.4 4.3 exponential_divide_fusion.2
  345.7 4.5 fusion.143
  350.2 6.3 fusion.145
  361.8 4.3 exponential_divide_fusion.2
  374.2 4.5 fusion.143
  378.6 6.3 fusion.145
  385.0 4.0 fusion.144
  390.9 4.3 exponential_divide_fusion.2
  403.2 4.4 fusion.143
  407.7 6.3 fusion.145
  413.9 4.0 fusion.144
  419.8 4.3 exponential_divide_fusion.2
  432.2 4.4 fusion.143
  436.6 6.3 fusion.145
  442.9 4.0 fusion.144
  454.5 9.2 all-to-all-done.6
  463.7 14.1 %all_to_all.134 = bf16[4,512,192]{1,2,0:T(8,128)(2,1)S(1)} all-to-all(bf16[4,512,192]{1,2,0:T(8,128)(2,1)S(1)} %copy.93), channel_id=1, replica_groups=mesh['fsdp'=8,'seq'=4] {'seq'}, dimensions={0} | all-to-all | bytes 1572864 | tf_op jit(solution)/shard_map/all_to_all | solution.py:221
  477.8 14.3 %all_to_all.135 = bf16[4,512,192]{1,2,0:T(8,128)(2,1)S(1)} all-to-all(bf16[4,512,192]{1,2,0:T(8,128)(2,1)S(1)} %bitcast.149), channel_id=1, replica_groups=mesh['fsdp'=8,'seq'=4] {'seq'}, dimensions={0} | all-to-all | bytes 1572864 | tf_op jit(solution)/shard_map/all_to_all | solution.py:219
  492.0 6.4 fusion.51
  499.5 8.2 fusion.82
  509.2 7.2 fusion.69
  519.1 37.6 %all-reduce.15 = (bf16[1536]{0:T(1024)(128)(2,1)S(1)}, bf16[768]{0:T(1024)(128)(2,1)S(1)}, bf16[768]{0:T(1024)(128)(2,1)S(1)}, bf16[768]{0:T(1024)(128)(2,1)S(1)...) all-reduce(f32[1536]{0:T(1024)S(1)} %pad_maximum_fusion.3, ...), channel_id=3, replica_groups=mesh['fsdp'=8,'seq'=4] {'fsdp'}, use_global_device_ids=true, to_apply=%region_22.23.clone | all-reduce | flops 9216 | bytes 55296
  559.2 66.9 %reduce-scatter.5.cloned.1.call-done = f32[96,2304]{1,0:T(8,128)} async-done(((f32[768,2304]{1,0:T(8,128)}), f32[96,2304]{1,0:T(8,128)}) %reduce-scatter.5.cloned.1.call-update) | async-done | bytes 884752 | tf_op jit(solution)/shard_map/reduce_scatter | solution.py:256
  628.1 164.6 %reduce-scatter.11.cloned.1.call-done = f32[384,768]{1,0:T(8,128)} async-done(((f32[3072,768]{1,0:T(8,128)}), f32[384,768]{1,0:T(8,128)}) %reduce-scatter.11.cloned.1.call-update) | async-done | bytes 1179664 | tf_op jit(solution)/shard_map/reduce_scatter | solution.py:264
  794.8 164.3 %reduce-scatter.9.cloned.1.call-done = f32[96,3072]{1,0:T(8,128)} async-done(((f32[768,3072]{1,0:T(8,128)}), f32[96,3072]{1,0:T(8,128)}) %reduce-scatter.9.cloned.1.call-update) | async-done | bytes 1179664 | tf_op jit(solution)/shard_map/reduce_scatter | solution.py:262
  961.4 5.6 broadcast_select_fusion
  968.2 14.3 %all-reduce.17 = (bf16[1,10,768]{2,1,0:T(8,128)(2,1)S(1)}, bf16[1,10,768]{2,1,0:T(8,128)(2,1)S(1)}, bf16[192]{0:T(256)(128)(2,1)S(1)}, bf16[96]{0:T(256)(128)(2,...) all-reduce(bf16[1,10,768]{2,1,0:T(8,128)(2,1)S(1)} %fusion.49, ...), channel_id=1, replica_groups=mesh['fsdp'=8,'seq'=4] {'seq'}, use_global_device_ids=true, to_apply=%region_16.17 | all-reduce | flops 16512 | bytes 66048 | tf_op jit(solution)/shard_map/psum | solution.py:297
  988.0 21.9 %all-reduce.21.cloned.1.call-done = (bf16[96,2304]{1,0:T(8,128)(2,1)}, bf16[96,768]{1,0:T(8,128)(2,1)}, bf16[96,3072]{1,0:T(8,128)(2,1)}, bf16[384,768]{1,0:T(8,128)(2,1)}) async-done(((bf16[96,2304]{1,0:T(8,128)(2,1)}, bf16[96,768]{1,0:T(8,128)(2,1)}, bf16[96,3072]{1,0:T(8,128)(2,1)}, bf16[384,768]{1,0:T(8,128)(2,1)}), (bf16[96,2304]{1,0:T(8,128)(2,1)}, bf16[96,768]{1,0:T(8,128)(2,1)}, ...) | async-done | bytes 1769488 | tf_op jit(solution)/shard_map/psum | solution.py:285
  (292 shorter events, 162.4 us)
Async XLA Ops:
  7.2 51.2 %copy-start = (bf16[1,10,768]{2,1,0:T(8,128)(2,1)S(1)}, bf16[1,10,768]{2,1,0:T(8,128)(2,1)}, u32[]{:S(2)}) copy-start(bf16[1,10,768]{2,1,0:T(8,128)(2,1)} %param.22) | copy-start | bytes 46084
  7.2 71.6 %all-gather.6.cloned.1.call-start = ((), (), s32[]{:S(2)}) async-start(), calls=%async_computation.12 | async-start | bytes 3981312 | tf_op jit(solution)/shard_map/all_gather | solution.py:79
  7.9 202.6 %all-gather.8.cloned.1.call-start = ((), (), s32[]{:S(2)}) async-start(), calls=%async_computation.13 | async-start | bytes 1327104 | tf_op jit(solution)/shard_map/all_gather | solution.py:81
  8.7 205.8 %all-gather.10.cloned.1.call-start = ((), (), s32[]{:S(2)}) async-start(), calls=%async_computation.14 | async-start | bytes 5308416 | tf_op jit(solution)/shard_map/all_gather | solution.py:133
  58.3 24.5 %copy-start.37 = (s32[10]{0:T(128)}, s32[10]{0:T(128)S(1)}, u32[]{:S(2)}) copy-start(s32[10]{0:T(128)S(1)} %iota_add_fusion.1) | copy-start | bytes 124
  58.4 24.4 %copy-start.43 = (pred[512]{0:T(512)(128)(4,1)}, pred[512]{0:T(512)(128)(4,1)S(1)}, u32[]{:S(2)}) copy-start(pred[512]{0:T(512)(128)(4,1)S(1)} %fusion.54) | copy-start | bytes 1540
  60.5 22.3 %copy-start.17 = (bf16[512,768]{1,0:T(8,128)(2,1)}, bf16[512,768]{1,0:T(8,128)(2,1)S(1)}, u32[]{:S(2)}) copy-start(bf16[512,768]{1,0:T(8,128)(2,1)S(1)} %fusion.47) | copy-start | bytes 2359300
  86.4 15.1 %all-to-all-start = ((bf16[512,4,192]{0,2,1:T(8,128)(2,1)}), bf16[512,4,192]{0,2,1:T(8,128)(2,1)S(1)}, u32[]{:S(2)}, u32[]{:S(2)}) async-start(bf16[512,4,192]{0,2,1:T(8,128)(2,1)} %bitcast.4), calls=%async_computation | async-start | bytes 1572864 | tf_op jit(solution)/shard_map/all_to_all | solution.py:92
  101.5 15.1 %all-to-all-start.2 = ((bf16[512,4,192]{0,2,1:T(8,128)(2,1)}), bf16[512,4,192]{0,2,1:T(8,128)(2,1)S(1)}, u32[]{:S(2)}, u32[]{:S(2)}) async-start(bf16[512,4,192]{0,2,1:T(8,128)(2,1)} %bitcast.8), calls=%async_computation.2 | async-start | bytes 1572864 | tf_op jit(solution)/shard_map/all_to_all | solution.py:94
  116.6 15.1 %all-to-all-start.1 = ((bf16[512,4,192]{0,2,1:T(8,128)(2,1)}), bf16[512,4,192]{0,2,1:T(8,128)(2,1)S(1)}, u32[]{:S(2)}, u32[]{:S(2)}) async-start(bf16[512,4,192]{0,2,1:T(8,128)(2,1)} %bitcast.6), calls=%async_computation.1 | async-start | bytes 1572864 | tf_op jit(solution)/shard_map/all_to_all | solution.py:93
  120.1 161.5 %all-gather.12.cloned.1.call-start = ((), (), s32[]{:S(2)}) async-start(), calls=%async_computation.15 | async-start | bytes 5308416 | tf_op jit(solution)/shard_map/all_gather | solution.py:135
  136.3 47.7 %copy-start.45 = (bf16[384]{0:T(512)(128)(2,1)S(1)}, bf16[384]{0:T(512)(128)(2,1)}, u32[]{:S(2)}) copy-start(bf16[384]{0:T(512)(128)(2,1)} %param.32) | copy-start | bytes 2308
  180.5 34.0 %copy-start.4 = (bf16[2048,3,64]{0,2,1:T(8,128)(2,1)}, bf16[2048,3,64]{0,2,1:T(8,128)(2,1)S(1)}, u32[]{:S(2)}) copy-start(bf16[2048,3,64]{0,2,1:T(8,128)(2,1)S(1)} %get-tuple-element.654) | copy-start | bytes 2359300
  180.5 34.0 %copy-start.6 = (bf16[2048,3,64]{0,2,1:T(8,128)(2,1)}, bf16[2048,3,64]{0,2,1:T(8,128)(2,1)S(1)}, u32[]{:S(2)}) copy-start(bf16[2048,3,64]{0,2,1:T(8,128)(2,1)S(1)} %get-tuple-element.655) | copy-start | bytes 2359300
  180.5 30.0 %all-to-all-start.3 = ((bf16[4,512,192]{1,2,0:T(8,128)(2,1)}), bf16[4,512,192]{1,2,0:T(8,128)(2,1)S(1)}, u32[]{:S(2)}, u32[]{:S(2)}) async-start(bf16[4,512,192]{1,2,0:T(8,128)(2,1)} %bitcast.10), calls=%async_computation.3 | async-start | bytes 1572864 | tf_op jit(solution)/shard_map/all_to_all | solution.py:124
  184.0 120.5 %copy-start.30 = (f32[768]{0:T(1024)}, f32[768]{0:T(1024)S(1)}, u32[]{:S(2)}) copy-start(f32[768]{0:T(1024)S(1)} %convert_element_type.215) | copy-start | bytes 9220
  184.1 97.5 %copy-start.39 = (f32[768]{0:T(1024)}, f32[768]{0:T(1024)S(1)}, u32[]{:S(2)}) copy-start(f32[768]{0:T(1024)S(1)} %convert_element_type.216) | copy-start | bytes 9220
  213.0 91.5 %copy-start.24 = (f32[512]{0:T(512)}, f32[512]{0:T(512)S(1)}, u32[]{:S(2)}) copy-start(f32[512]{0:T(512)S(1)} %broadcast_multiply_fusion.1) | copy-start | bytes 6148
  214.5 90.1 %copy-start.33 = (f32[512]{0:T(512)}, f32[512]{0:T(512)S(1)}, u32[]{:S(2)}) copy-start(f32[512]{0:T(512)S(1)} %fusion.65) | copy-start | bytes 6148
  214.5 67.1 %copy-start.8 = (f32[512,768]{1,0:T(8,128)S(1)}, f32[512,768]{1,0:T(8,128)}, u32[]{:S(2)}) copy-start(f32[512,768]{1,0:T(8,128)} %copy-done.7) | copy-start | bytes 4718596
  281.6 6.5 copy-start.13
  291.1 9.8 slice-start
  291.9 9.0 copy-start.18
  292.0 8.9 slice-start.1
  307.2 6.2 copy-start.15
  309.1 15.9 %all-to-all-start.4 = ((bf16[512,4,192]{0,2,1:T(8,128)(2,1)}), bf16[512,4,192]{0,2,1:T(8,128)(2,1)}, u32[]{:S(2)}, u32[]{:S(2)}) async-start(bf16[512,4,192]{0,2,1:T(8,128)(2,1)} %bitcast.15), calls=%async_computation.4 | async-start | bytes 1572864 | tf_op jit(solution)/shard_map/all_to_all | solution.py:177
  313.4 244.0 %reduce-scatter.7.cloned.1.call-start = ((), (), s32[]{:S(2)}) async-start(), calls=%async_computation.17 | async-start | bytes 2654208 | tf_op jit(solution)/shard_map/reduce_scatter | solution.py:258
  316.8 14.6 %copy-start.5 = (bf16[2048,3,64]{0,2,1:T(8,128)(2,1)S(1)}, bf16[2048,3,64]{0,2,1:T(8,128)(2,1)}, u32[]{:S(2)}) copy-start(bf16[2048,3,64]{0,2,1:T(8,128)(2,1)} %copy-done.4) | copy-start | bytes 2359300
  337.7 4.5 copy-start.2
  345.7 10.8 %copy-start.3 = (f32[3,512,2048]{2,1,0:T(8,128)S(1)}, f32[3,512,2048]{2,1,0:T(8,128)}, u32[]{:S(2)}) copy-start(f32[3,512,2048]{2,1,0:T(8,128)} %copy-done.2) | copy-start | bytes 37748740 | tf_op jit(solution)/shard_map/while
  374.2 10.8 %copy-start.3 = (f32[3,512,2048]{2,1,0:T(8,128)S(1)}, f32[3,512,2048]{2,1,0:T(8,128)}, u32[]{:S(2)}) copy-start(f32[3,512,2048]{2,1,0:T(8,128)} %copy-done.2) | copy-start | bytes 37748740 | tf_op jit(solution)/shard_map/while
  395.2 4.5 copy-start.2
  403.2 10.7 %copy-start.3 = (f32[3,512,2048]{2,1,0:T(8,128)S(1)}, f32[3,512,2048]{2,1,0:T(8,128)}, u32[]{:S(2)}) copy-start(f32[3,512,2048]{2,1,0:T(8,128)} %copy-done.2) | copy-start | bytes 37748740 | tf_op jit(solution)/shard_map/while
  432.2 10.7 %copy-start.3 = (f32[3,512,2048]{2,1,0:T(8,128)S(1)}, f32[3,512,2048]{2,1,0:T(8,128)}, u32[]{:S(2)}) copy-start(f32[3,512,2048]{2,1,0:T(8,128)} %copy-done.2) | copy-start | bytes 37748740 | tf_op jit(solution)/shard_map/while
  448.6 15.1 %all-to-all-start.6 = ((bf16[4,512,192]{1,2,0:T(8,128)(2,1)}), bf16[4,512,192]{1,2,0:T(8,128)(2,1)S(1)}, u32[]{:S(2)}, u32[]{:S(2)}) async-start(bf16[4,512,192]{1,2,0:T(8,128)(2,1)} %copy.92), calls=%async_computation.6 | async-start | bytes 1572864 | tf_op jit(solution)/shard_map/all_to_all | solution.py:220
  452.1 174.0 %reduce-scatter.5.cloned.1.call-start = ((), (), s32[]{:S(2)}) async-start(), calls=%async_computation.16 | async-start | bytes 7962624 | tf_op jit(solution)/shard_map/reduce_scatter | solution.py:256
  452.1 25.6 %copy-start.14 = (bf16[4,512,3,64]{1,3,2,0:T(8,128)(2,1)S(1)}, bf16[4,512,3,64]{1,3,2,0:T(8,128)(2,1)}, u32[]{:S(2)}) copy-start(bf16[4,512,3,64]{1,3,2,0:T(8,128)(2,1)} %get-tuple-element.132) | copy-start | bytes 2359300
  463.7 14.1 %copy-start.16 = (bf16[4,512,192]{1,2,0:T(8,128)(2,1)}, bf16[4,512,192]{1,2,0:T(8,128)(2,1)S(1)}, u32[]{:S(2)}) copy-start(bf16[4,512,192]{1,2,0:T(8,128)(2,1)S(1)} %all-to-all-done.6) | copy-start | bytes 2359300
  498.4 294.3 %reduce-scatter.11.cloned.1.call-start = ((), (), s32[]{:S(2)}) async-start(), calls=%async_computation.19 | async-start | bytes 10616832 | tf_op jit(solution)/shard_map/reduce_scatter | solution.py:264
  507.8 451.4 %reduce-scatter.9.cloned.1.call-start = ((), (), s32[]{:S(2)}) async-start(), calls=%async_computation.18 | async-start | bytes 10616832 | tf_op jit(solution)/shard_map/reduce_scatter | solution.py:262
  516.5 493.4 %all-reduce.21.cloned.1.call-start = ((), (), s32[]{:S(2)}) async-start(), calls=%async_computation.20 | async-start | bytes 3538944 | tf_op jit(solution)/shard_map/psum | solution.py:285
  557.4 404.0 %copy-start.11 = (f32[512,768]{1,0:T(8,128)S(1)}, f32[512,768]{1,0:T(8,128)}, u32[]{:S(2)}) copy-start(f32[512,768]{1,0:T(8,128)} %copy-done.10) | copy-start | bytes 4718596
  557.4 404.0 %copy-start.36 = (f32[512]{0:T(512)S(1)}, f32[512]{0:T(512)}, u32[]{:S(2)}) copy-start(f32[512]{0:T(512)} %copy-done.35) | copy-start | bytes 6148
  557.4 404.0 %copy-start.44 = (pred[512]{0:T(512)(128)(4,1)S(1)}, pred[512]{0:T(512)(128)(4,1)}, u32[]{:S(2)}) copy-start(pred[512]{0:T(512)(128)(4,1)} %copy-done.43) | copy-start | bytes 1540
  961.4 5.6 copy-start.23
  961.4 6.2 copy-start.38
  967.0 49.1 %copy-start.1 = (bf16[1,10,768]{2,1,0:T(8,128)(2,1)S(1)}, bf16[1,10,768]{2,1,0:T(8,128)(2,1)}, u32[]{:S(2)}) copy-start(bf16[1,10,768]{2,1,0:T(8,128)(2,1)} %param.22) | copy-start | bytes 46084
  1009.9 5.4 copy-start.21
  (24 other events, 58.3 us)
Sparse Core Ops, SparseCore 0:
  10.2 68.4 all-gather.5
  80.9 39.4 all-gather.7
  122.7 78.6 all-gather.9
  203.4 78.1 all-gather.11
  317.4 67.6 reduce-scatter.6
  498.5 127.5 reduce-scatter.4
  630.1 162.5 reduce-scatter.10
  796.7 162.3 reduce-scatter.8
  963.1 46.7 all-reduce.20
where the time goes:
time: 1030 us; the launch traced here: 1020 us
  waiting for transfers between devices  528 us (51%)
  matrix products  195 us (19%)
  blocking collectives  146 us (14%)
  other arithmetic  57.2 us (6%)
  local copies, waits for them, and re-layouts  50.3 us (5%)
  starting transfers between devices  22.2 us (2%)
  between operations  18.7 us (2%)
    reduce_scatter x1, waiting for transfers between devices, per_device(): lax.psum_scatter(grad_down_weight, 'fsdp', scatter_dimension=0, tiled=True)  165 us
    reduce_scatter x1, waiting for transfers between devices, per_device(): lax.psum_scatter(grad_up_weight, 'fsdp', scatter_dimension=0, tiled=True)  164 us
    unnamed x2, blocking collectives  77.3 us
    reduce_scatter x1, waiting for transfers between devices, per_device(): lax.psum_scatter(grad_qkv_weight, 'fsdp', scatter_dimension=0, tiled=True)  66.9 us
    all_gather x1, waiting for transfers between devices, per_device(): lax.all_gather(down_weight, 'fsdp', axis=0, tiled=True)  46.2 us
    all_gather x1, blocking collectives, per_device(): lax.all_gather(up_bias, 'fsdp', axis=0, tiled=True)  26.3 us
    dot_general x8, matrix products, scores_for(): jnp.einsum('qhd,khd->hqk', query_block, heads_key, preferred_element_type...  25.4 us
    dot_general x4, matrix products, over_rows(): lax.dot_general(left, right, (((0,), (0,)), ((), ())), preferred_element_...  25.2 us
  transfers between devices with their start and end apart: 15, of which 11 were waited for; matrix products, arithmetic and copies ran while one was open for 25% of the time, Pallas kernels for 0%

commit v1 on v0

--- a/solution.py
+++ b/solution.py
@@ -8,6 +8,28 @@
 MEM = 10
 norm_epsilon = 1e-06
 masked_score = -1e30
+
+
+def in_order(blocks, dim):
+    blocks = jnp.moveaxis(blocks, 0, dim)
+    lengths = blocks.shape
+    return blocks.reshape(*lengths[:dim], lengths[dim] * lengths[dim + 1], *lengths[dim + 2 :])
+
+
+def ring_gather(x, axis, dim):
+    size = lax.axis_size(axis)
+    pairs = [(i, (i + 1) % size) for i in range(size)]
+    back = [(b, a) for a, b in pairs]
+    lower, upper = ([], [])
+    for hop in range(size - 1):
+        if hop % 2 == 0:
+            lower.append(lax.ppermute(lower[-1] if lower else x, axis, pairs))
+        else:
+            upper.append(lax.ppermute(upper[-1] if upper else x, axis, back))
+    blocks = jnp.stack([*lower[::-1], x, *upper])
+    shift = lax.axis_index(axis) - len(lower)
+    blocks = blocks[(jnp.arange(size) - shift) % size]
+    return in_order(blocks, dim)
 
 
 def normalize(values, gain_vec, shift_vec):
@@ -132,7 +154,7 @@
     up_full, up_bias_full, down_full, down_bias_full, gain_two, shift_two = (
         lax.all_gather(up_weight, "fsdp", axis=0, tiled=True),
         lax.all_gather(up_bias, "fsdp", axis=0, tiled=True),
-        lax.all_gather(down_weight, "fsdp", axis=0, tiled=True),
+        ring_gather(down_weight, "fsdp", 0),
         lax.all_gather(down_bias, "fsdp", axis=0, tiled=True),
         lax.all_gather(norm2_gain, "fsdp", axis=0, tiled=True),
         lax.all_gather(norm2_bias, "fsdp", axis=0, tiled=True),

time: 1030 us -> 1070 us (1.039)
  blocking collectives: 146 us -> 176 us
  waiting for transfers between devices: 528 us -> 503 us
  local copies, waits for them, and re-layouts: 50.3 us -> 69 us
  starting transfers between devices: 22.2 us -> 37.4 us
    ppermute x0 -> x7, waiting for transfers between devices: none -> 22.7 us  [the longest x4 22.7 us: ring_gather(): lower.append(lax.ppermute(lower[-1] if lower else x, axis, pairs))]
    all_gather x1, blocking collectives: 26.3 us -> 46.4 us  [per_device(): lax.all_gather(up_bias, 'fsdp', axis=0, tiled=True)]
    all_gather x1, waiting for transfers between devices: 18.2 us -> 0.01 us  [per_device(): lax.all_gather(qkv_weight, 'fsdp', axis=0, tiled=True)]
    ppermute x0 -> x7, starting transfers between devices: none -> 14.6 us  [the longest x3 11.6 us: ring_gather(): upper.append(lax.ppermute(upper[-1] if upper else x, axis, back))]
    unnamed x124 -> x143, local copies, waits for them, and re-layouts: 16.2 us -> 27.3 us
  transfers between devices with their start and end apart: 15 -> 22, of which waited for: 11 -> 11; matrix products, arithmetic and copies ran while one was open for 25% -> 27% of each run, Pallas kernels for 0% -> 0%
where the time goes in v1:
time: 1070 us
  waiting for transfers between devices  503 us (47%)
  matrix products  195 us (18%)
  blocking collectives  176 us (16%)
  local copies, waits for them, and re-layouts  69 us (6%)
  other arithmetic  60.4 us (6%)
  starting transfers between devices  37.4 us (3%)
  between operations  18.9 us (2%)
    reduce_scatter x1, waiting for transfers between devices, per_device(): lax.psum_scatter(grad_down_weight, 'fsdp', scatter_dimension=0, tiled=True)  164 us
    reduce_scatter x1, waiting for transfers between devices, per_device(): lax.psum_scatter(grad_up_weight, 'fsdp', scatter_dimension=0, tiled=True)  164 us
    unnamed x2, blocking collectives  87.4 us
    reduce_scatter x1, waiting for transfers between devices, per_device(): lax.psum_scatter(grad_qkv_weight, 'fsdp', scatter_dimension=0, tiled=True)  67.1 us
    all_gather x1, blocking collectives, per_device(): lax.all_gather(up_bias, 'fsdp', axis=0, tiled=True)  46.4 us
    all_gather x1, waiting for transfers between devices, per_device(): lax.all_gather(down_weight, 'fsdp', axis=0, tiled=True)  38.8 us
    unnamed x143, local copies, waits for them, and re-layouts  27.3 us
    dot_general x4, matrix products, over_rows(): lax.dot_general(left, right, (((0,), (0,)), ((), ())), preferred_element_...  25.4 us
  transfers between devices with their start and end apart: 22, of which 11 were waited for; matrix products, arithmetic and copies ran while one was open for 27% of the time, Pallas kernels for 0%

profile of v1, /device:TPU:0, one launch (start us, length us, event | category | flops | bytes accessed | tf_op | source)
XLA Modules:
  0.0 1065.2 jit_solution(6285369589855746505)
XLA Ops:
  24.7 49.9 %all-reduce.16 = (bf16[1536]{0:T(1024)(128)(2,1)S(1)}, bf16[768]{0:T(1024)(128)(2,1)S(1)}, bf16[768]{0:T(1024)(128)(2,1)S(1)}, bf16[768]{0:T(1024)(128)(2,1)S(1)...) all-reduce(bf16[1536]{0:T(1024)(128)(2,1)S(1)} %dynamic-update-slic, ...), channel_id=1, replica_groups=mesh['fsdp'=8,'seq'=4] {'fsdp'}, use_global_device_ids=true, to_apply=%add | all-reduce | flops 6144 | bytes 24576
  76.8 22.7 %collective-permute-done.1 = bf16[384,768]{1,0:T(8,128)(2,1)S(1)} collective-permute-done((bf16[384,768]{1,0:T(8,128)(2,1)S(1)}, bf16[384,768]{1,0:T(8,128)(2,1)S(1)}, u32[]{:S(2)}, u32[]{:S(2)}) %collective-permute-start.1) | collective-permute-done | bytes 589856 | tf_op jit(solution)/shard_map/ppermute | solution.py:26
  99.5 4.2 fusion.82
  111.0 4.6 collective-permute-start.5
  115.7 46.4 %all-gather = bf16[8,1,384]{2,1,0:T(2,128)(2,1)S(1)} all-gather(bf16[1,1,384]{2,1,0:T(2,128)(2,1)S(1)} %reshape.265), channel_id=1, replica_groups=mesh['fsdp'=8,'seq'=4] {'fsdp'}, dimensions={0}, use_global_device_ids=true | all-gather | bytes 6912 | tf_op jit(solution)/shard_map/all_gather | solution.py:156
  169.1 3.9 collective-permute-start.6
  200.0 44.2 %while.30 = (s32[]{:T(128)}, bf16[4,512,3,64]{1,3,2,0:T(8,128)(2,1)}, f32[4,3,512,1]{2,1,3,0:T(4,128)S(1)}, f32[4,3,512,1]{2,1,3,0:T(4,128)S(1)}, s32[4]{0:T(128...) while((s32[]{:T(128)}, ...), condition=%wide.region_4.5_spmd.clone, body=%wide.region_1.4_spmd.clone.sunk | while | flops 843152384 | bytes 39787204 | solution.py:142
  206.7 4.3 fusion.135
  217.8 4.3 fusion.135
  228.8 4.3 fusion.135
  239.9 4.3 fusion.135
  244.2 3.9 all-to-all-start.3
  254.0 5.6 gather_fusion
  262.8 19.6 %multiply_convert_fusion.1 = (bf16[512,3072]{1,0:T(8,128)(2,1)S(1)}, f32[512,3072]{1,0:T(8,128)}, f32[512,3072]{1,0:T(8,128)}) fusion(f32[3072]{0:T(1024)S(1)} %bitcast.174, bf16[768,3072]{1,0:T(8,128)(2,1)} %all-gather.10.cloned.1.call-done, f32[512,768]{1,0:T(8,128)S(1)} %get-tuple-element.399, f32[768]{0:T(1024)S(1)} %convert_element_type.216, ...), kind=kOutput, calls=%fused_computation.50 | convolution fusion | flops 2521694208 | bytes 22042624 | tf_op jit(solution)/shard_map/dot_general | solution.py:163
  289.6 38.8 %all-gather.12.cloned.1.call-done = bf16[3072,768]{1,0:T(8,128)(2,1)} async-done(((bf16[384,768]{1,0:T(8,128)(2,1)}), bf16[3072,768]{1,0:T(8,128)(2,1)}) %all-gather.12.cloned.1.call-update) | async-done | bytes 4718608 | tf_op jit(solution)/shard_map/all_gather | solution.py:177
  328.4 9.5 convert_reduce_fusion
  337.9 7.2 multiply_reduce_fusion.2
  350.5 4.2 all-to-all-start.4
  358.4 8.0 all-to-all-done.4
  372.8 115.5 %while.31 = (s32[]{:T(128)}, f32[2048,3,64]{0,2,1:T(8,128)S(1)}, f32[2048,3,64]{0,2,1:T(8,128)}, bf16[4,512,3,64]{1,3,2,0:T(8,128)(2,1)}, s32[4]{0:T(128)S(1)}, ...) while((s32[]{:T(128)}, f32[2048,3,64]{0,2,1:T(8,128)S(1)}, ...), condition=%wide.region_15.16_spmd.clone, body=%wide.region_13.15_spmd.clone.sunk | while | flops 2046886400 | bytes 204722992 | solution.py:232
  374.7 4.3 exponential_divide_fusion.2
  387.1 4.5 fusion.145
  391.6 6.3 fusion.147
  403.2 4.3 exponential_divide_fusion.2
  415.6 4.5 fusion.145
  420.1 6.3 fusion.147
  426.4 4.0 fusion.146
  432.3 4.3 exponential_divide_fusion.2
  444.7 4.4 fusion.145
  449.1 6.3 fusion.147
  455.4 4.0 fusion.146
  461.3 4.3 exponential_divide_fusion.2
  473.7 4.4 fusion.145
  478.1 6.3 fusion.147
  484.4 4.0 fusion.146
  496.0 9.3 all-to-all-done.6
  505.3 14.1 %all_to_all.134 = bf16[4,512,192]{1,2,0:T(8,128)(2,1)S(1)} all-to-all(bf16[4,512,192]{1,2,0:T(8,128)(2,1)S(1)} %copy.93), channel_id=1, replica_groups=mesh['fsdp'=8,'seq'=4] {'seq'}, dimensions={0} | all-to-all | bytes 1572864 | tf_op jit(solution)/shard_map/all_to_all | solution.py:243
  519.4 14.3 %all_to_all.135 = bf16[4,512,192]{1,2,0:T(8,128)(2,1)S(1)} all-to-all(bf16[4,512,192]{1,2,0:T(8,128)(2,1)S(1)} %bitcast.169), channel_id=1, replica_groups=mesh['fsdp'=8,'seq'=4] {'seq'}, dimensions={0} | all-to-all | bytes 1572864 | tf_op jit(solution)/shard_map/all_to_all | solution.py:241
  533.6 6.4 fusion.51
  541.2 8.2 fusion.84
  550.8 7.2 fusion.71
  560.9 37.5 %all-reduce.15 = (bf16[1536]{0:T(1024)(128)(2,1)S(1)}, bf16[768]{0:T(1024)(128)(2,1)S(1)}, bf16[768]{0:T(1024)(128)(2,1)S(1)}, bf16[768]{0:T(1024)(128)(2,1)S(1)...) all-reduce(f32[1536]{0:T(1024)S(1)} %pad_maximum_fusion.3, ...), channel_id=3, replica_groups=mesh['fsdp'=8,'seq'=4] {'fsdp'}, use_global_device_ids=true, to_apply=%region_22.23.clone | all-reduce | flops 9216 | bytes 55296
  600.7 67.1 %reduce-scatter.5.cloned.1.call-done = f32[96,2304]{1,0:T(8,128)} async-done(((f32[768,2304]{1,0:T(8,128)}), f32[96,2304]{1,0:T(8,128)}) %reduce-scatter.5.cloned.1.call-update) | async-done | bytes 884752 | tf_op jit(solution)/shard_map/reduce_scatter | solution.py:278
  669.7 164.4 %reduce-scatter.11.cloned.1.call-done = f32[384,768]{1,0:T(8,128)} async-done(((f32[3072,768]{1,0:T(8,128)}), f32[384,768]{1,0:T(8,128)}) %reduce-scatter.11.cloned.1.call-update) | async-done | bytes 1179664 | tf_op jit(solution)/shard_map/reduce_scatter | solution.py:286
  836.3 164.3 %reduce-scatter.9.cloned.1.call-done = f32[96,3072]{1,0:T(8,128)} async-done(((f32[768,3072]{1,0:T(8,128)}), f32[96,3072]{1,0:T(8,128)}) %reduce-scatter.9.cloned.1.call-update) | async-done | bytes 1179664 | tf_op jit(solution)/shard_map/reduce_scatter | solution.py:284
  1002.9 5.6 broadcast_select_fusion
  1009.7 14.3 %all-reduce.17 = (bf16[1,10,768]{2,1,0:T(8,128)(2,1)S(1)}, bf16[1,10,768]{2,1,0:T(8,128)(2,1)S(1)}, bf16[192]{0:T(256)(128)(2,1)S(1)}, bf16[96]{0:T(256)(128)(2,...) all-reduce(bf16[1,10,768]{2,1,0:T(8,128)(2,1)S(1)} %fusion.49, ...), channel_id=1, replica_groups=mesh['fsdp'=8,'seq'=4] {'seq'}, use_global_device_ids=true, to_apply=%region_16.17 | all-reduce | flops 16512 | bytes 66048 | tf_op jit(solution)/shard_map/psum | solution.py:319
  1029.4 21.9 %all-reduce.21.cloned.1.call-done = (bf16[96,2304]{1,0:T(8,128)(2,1)}, bf16[96,768]{1,0:T(8,128)(2,1)}, bf16[96,3072]{1,0:T(8,128)(2,1)}, bf16[384,768]{1,0:T(8,128)(2,1)}) async-done(((bf16[96,2304]{1,0:T(8,128)(2,1)}, bf16[96,768]{1,0:T(8,128)(2,1)}, bf16[96,3072]{1,0:T(8,128)(2,1)}, bf16[384,768]{1,0:T(8,128)(2,1)}), (bf16[96,2304]{1,0:T(8,128)(2,1)}, bf16[96,768]{1,0:T(8,128)(2,1)}, ...) | async-done | bytes 1769488 | tf_op jit(solution)/shard_map/psum | solution.py:307
  (328 shorter events, 188.3 us)
Async XLA Ops:
  7.2 67.6 %copy-start = (bf16[1,10,768]{2,1,0:T(8,128)(2,1)S(1)}, bf16[1,10,768]{2,1,0:T(8,128)(2,1)}, u32[]{:S(2)}) copy-start(bf16[1,10,768]{2,1,0:T(8,128)(2,1)} %param.22) | copy-start | bytes 46084
  7.2 92.3 %all-gather.6.cloned.1.call-start = ((), (), s32[]{:S(2)}) async-start(), calls=%async_computation.12 | async-start | bytes 3981312 | tf_op jit(solution)/shard_map/all_gather | solution.py:101
  7.9 251.6 %all-gather.8.cloned.1.call-start = ((), (), s32[]{:S(2)}) async-start(), calls=%async_computation.13 | async-start | bytes 1327104 | tf_op jit(solution)/shard_map/all_gather | solution.py:103
  8.7 254.1 %all-gather.10.cloned.1.call-start = ((), (), s32[]{:S(2)}) async-start(), calls=%async_computation.14 | async-start | bytes 5308416 | tf_op jit(solution)/shard_map/all_gather | solution.py:155
  9.4 65.1 %collective-permute-start = (bf16[384,768]{1,0:T(8,128)(2,1)}, bf16[384,768]{1,0:T(8,128)(2,1)S(1)}, u32[]{:S(2)}, u32[]{:S(2)}) collective-permute-start(bf16[384,768]{1,0:T(8,128)(2,1)} %param.33), channel_id=1, source_target_pairs={{0,4},{4,8},{8,12},{12,16},{16,20},{20,24},{24,28},{28,0},{1,5},{5... | collective-permute-start | bytes 1769480 | tf_op jit(solution)/shard_map/ppermute | solution.py:26
  12.4 98.5 %collective-permute-start.4 = (bf16[384,768]{1,0:T(8,128)(2,1)}, bf16[384,768]{1,0:T(8,128)(2,1)S(1)}, u32[]{:S(2)}, u32[]{:S(2)}) collective-permute-start(bf16[384,768]{1,0:T(8,128)(2,1)} %param.33), channel_id=1, source_target_pairs={{4,0},{8,4},{12,8},{16,12},{20,16},{24,20},{28,24},{0,28},{5,1},{9... | collective-permute-start | bytes 1769480 | tf_op jit(solution)/shard_map/ppermute | solution.py:28
  74.5 29.2 %copy-start.43 = (s32[10]{0:T(128)}, s32[10]{0:T(128)S(1)}, u32[]{:S(2)}) copy-start(s32[10]{0:T(128)S(1)} %iota_add_fusion.1) | copy-start | bytes 124
  74.5 29.2 %copy-start.26 = (s32[512]{0:T(512)}, s32[512]{0:T(512)S(1)}, u32[]{:S(2)}) copy-start(s32[512]{0:T(512)S(1)} %iota_add_fusion) | copy-start | bytes 6148
  74.6 29.2 %copy-start.23 = (bf16[384,768]{1,0:T(8,128)(2,1)}, bf16[384,768]{1,0:T(8,128)(2,1)S(1)}, u32[]{:S(2)}) copy-start(bf16[384,768]{1,0:T(8,128)(2,1)S(1)} %collective-permute-done) | copy-start | bytes 1769476
  74.6 25.0 %collective-permute-start.1 = (bf16[384,768]{1,0:T(8,128)(2,1)S(1)}, bf16[384,768]{1,0:T(8,128)(2,1)S(1)}, u32[]{:S(2)}, u32[]{:S(2)}) collective-permute-start(bf16[384,768]{1,0:T(8,128)(2,1)S(1)} %collective-permute-done), channel_id=1, source_target_pairs={{0,4},{4,8},{8,12},{12,16},{16,20},{20,24},{24,28},{28,0},{1,5},{5... | collective-permute-start | bytes 1769480 | tf_op jit(solution)/shard_map/ppermute | solution.py:26
  74.7 29.1 %copy-start.51 = (pred[512]{0:T(512)(128)(4,1)}, pred[512]{0:T(512)(128)(4,1)S(1)}, u32[]{:S(2)}) copy-start(pred[512]{0:T(512)(128)(4,1)S(1)} %fusion.54) | copy-start | bytes 1540
  76.8 27.0 %copy-start.19 = (bf16[512,768]{1,0:T(8,128)(2,1)}, bf16[512,768]{1,0:T(8,128)(2,1)S(1)}, u32[]{:S(2)}) copy-start(bf16[512,768]{1,0:T(8,128)(2,1)S(1)} %fusion.47) | copy-start | bytes 2359300
  99.5 16.0 %collective-permute-start.2 = (bf16[384,768]{1,0:T(8,128)(2,1)S(1)}, bf16[384,768]{1,0:T(8,128)(2,1)S(1)}, u32[]{:S(2)}, u32[]{:S(2)}) collective-permute-start(bf16[384,768]{1,0:T(8,128)(2,1)S(1)} %collective-permute-done.1), channel_id=1, source_target_pairs={{0,4},{4,8},{8,12},{12,16},{16,20},{20,24},{24,28},{28,0},{1,5},{5... | collective-permute-start | bytes 1769480 | tf_op jit(solution)/shard_map/ppermute | solution.py:26
  107.4 57.7 %all-to-all-start = ((bf16[512,4,192]{0,2,1:T(8,128)(2,1)}), bf16[512,4,192]{0,2,1:T(8,128)(2,1)S(1)}, u32[]{:S(2)}, u32[]{:S(2)}) async-start(bf16[512,4,192]{0,2,1:T(8,128)(2,1)} %bitcast.4), calls=%async_computation | async-start | bytes 1572864 | tf_op jit(solution)/shard_map/all_to_all | solution.py:114
  110.9 217.5 %all-gather.12.cloned.1.call-start = ((), (), s32[]{:S(2)}) async-start(), calls=%async_computation.15 | async-start | bytes 5308416 | tf_op jit(solution)/shard_map/all_gather | solution.py:177
  111.0 62.9 %copy-start.22 = (bf16[384,768]{1,0:T(8,128)(2,1)}, bf16[384,768]{1,0:T(8,128)(2,1)S(1)}, u32[]{:S(2)}) copy-start(bf16[384,768]{1,0:T(8,128)(2,1)S(1)} %collective-permute-done.4) | copy-start | bytes 1769476
  111.0 58.1 %collective-permute-start.5 = (bf16[384,768]{1,0:T(8,128)(2,1)S(1)}, bf16[384,768]{1,0:T(8,128)(2,1)}, u32[]{:S(2)}, u32[]{:S(2)}) collective-permute-start(bf16[384,768]{1,0:T(8,128)(2,1)S(1)} %collective-permute-done.4), channel_id=1, source_target_pairs={{4,0},{8,4},{12,8},{16,12},{20,16},{24,20},{28,24},{0,28},{5,1},{9... | collective-permute-start | bytes 1769480 | tf_op jit(solution)/shard_map/ppermute | solution.py:28
  115.5 57.5 %collective-permute-start.3 = (bf16[384,768]{1,0:T(8,128)(2,1)S(1)}, bf16[384,768]{1,0:T(8,128)(2,1)S(1)}, u32[]{:S(2)}, u32[]{:S(2)}) collective-permute-start(bf16[384,768]{1,0:T(8,128)(2,1)S(1)} %collective-permute-done.2), channel_id=1, source_target_pairs={{0,4},{4,8},{8,12},{12,16},{16,20},{20,24},{24,28},{28,0},{1,5},{5... | collective-permute-start | bytes 1769480 | tf_op jit(solution)/shard_map/ppermute | solution.py:26
  115.6 229.5 %copy-start.36 = (f32[768]{0:T(1024)}, f32[768]{0:T(1024)S(1)}, u32[]{:S(2)}) copy-start(f32[768]{0:T(1024)S(1)} %convert_element_type.215) | copy-start | bytes 9220
  115.6 166.9 %copy-start.45 = (f32[768]{0:T(1024)}, f32[768]{0:T(1024)S(1)}, u32[]{:S(2)}) copy-start(f32[768]{0:T(1024)S(1)} %convert_element_type.216) | copy-start | bytes 9220
  165.1 15.1 %all-to-all-start.2 = ((bf16[512,4,192]{0,2,1:T(8,128)(2,1)}), bf16[512,4,192]{0,2,1:T(8,128)(2,1)S(1)}, u32[]{:S(2)}, u32[]{:S(2)}) async-start(bf16[512,4,192]{0,2,1:T(8,128)(2,1)} %bitcast.8), calls=%async_computation.2 | async-start | bytes 1572864 | tf_op jit(solution)/shard_map/all_to_all | solution.py:116
  169.1 83.0 %collective-permute-start.6 = (bf16[384,768]{1,0:T(8,128)(2,1)}, bf16[384,768]{1,0:T(8,128)(2,1)}, u32[]{:S(2)}, u32[]{:S(2)}) collective-permute-start(bf16[384,768]{1,0:T(8,128)(2,1)} %collective-permute-done.5), channel_id=1, source_target_pairs={{4,0},{8,4},{12,8},{16,12},{20,16},{24,20},{28,24},{0,28},{5,1},{9... | collective-permute-start | bytes 1769480 | tf_op jit(solution)/shard_map/ppermute | solution.py:28
  180.2 15.3 %all-to-all-start.1 = ((bf16[512,4,192]{0,2,1:T(8,128)(2,1)}), bf16[512,4,192]{0,2,1:T(8,128)(2,1)S(1)}, u32[]{:S(2)}, u32[]{:S(2)}) async-start(bf16[512,4,192]{0,2,1:T(8,128)(2,1)} %bitcast.6), calls=%async_computation.1 | async-start | bytes 1572864 | tf_op jit(solution)/shard_map/all_to_all | solution.py:115
  244.2 15.4 %copy-start.4 = (bf16[2048,3,64]{0,2,1:T(8,128)(2,1)}, bf16[2048,3,64]{0,2,1:T(8,128)(2,1)S(1)}, u32[]{:S(2)}) copy-start(bf16[2048,3,64]{0,2,1:T(8,128)(2,1)S(1)} %get-tuple-element.654) | copy-start | bytes 2359300
  244.2 15.4 %copy-start.6 = (bf16[2048,3,64]{0,2,1:T(8,128)(2,1)}, bf16[2048,3,64]{0,2,1:T(8,128)(2,1)S(1)}, u32[]{:S(2)}) copy-start(bf16[2048,3,64]{0,2,1:T(8,128)(2,1)S(1)} %get-tuple-element.655) | copy-start | bytes 2359300
  244.2 15.5 %all-to-all-start.3 = ((bf16[4,512,192]{1,2,0:T(8,128)(2,1)}), bf16[4,512,192]{1,2,0:T(8,128)(2,1)S(1)}, u32[]{:S(2)}, u32[]{:S(2)}) async-start(bf16[4,512,192]{1,2,0:T(8,128)(2,1)} %bitcast.10), calls=%async_computation.3 | async-start | bytes 1572864 | tf_op jit(solution)/shard_map/all_to_all | solution.py:146
  259.7 22.8 %copy-start.16 = (bf16[4,512,192]{1,2,0:T(8,128)(2,1)}, bf16[4,512,192]{1,2,0:T(8,128)(2,1)S(1)}, u32[]{:S(2)}) copy-start(bf16[4,512,192]{1,2,0:T(8,128)(2,1)S(1)} %all-to-all-done.3) | copy-start | bytes 2359300
  262.4 20.1 %copy-start.7 = (f32[512,768]{1,0:T(8,128)}, f32[512,768]{1,0:T(8,128)S(1)}, u32[]{:S(2)}) copy-start(f32[512,768]{1,0:T(8,128)S(1)} %get-tuple-element.399) | copy-start | bytes 4718596
  262.4 82.7 %copy-start.29 = (f32[512]{0:T(512)}, f32[512]{0:T(512)S(1)}, u32[]{:S(2)}) copy-start(f32[512]{0:T(512)S(1)} %broadcast_multiply_fusion.1) | copy-start | bytes 6148
  262.8 82.3 %copy-start.39 = (f32[512]{0:T(512)}, f32[512]{0:T(512)S(1)}, u32[]{:S(2)}) copy-start(f32[512]{0:T(512)S(1)} %fusion.65) | copy-start | bytes 6148
  262.8 19.7 %copy-start.12 = (bf16[8,384,768]{2,1,0:T(8,128)(2,1)S(1)}, bf16[8,384,768]{2,1,0:T(8,128)(2,1)}, u32[]{:S(2)}) copy-start(bf16[8,384,768]{2,1,0:T(8,128)(2,1)} %gather_fusion) | copy-start | bytes 14155780
  262.8 19.7 %copy-start.47 = (f32[768]{0:T(1024)S(1)}, f32[768]{0:T(1024)}, u32[]{:S(2)}) copy-start(f32[768]{0:T(1024)} %convert_element_type.220) | copy-start | bytes 9220
  289.6 48.3 %copy-start.20 = (bf16[512,768]{1,0:T(8,128)(2,1)}, bf16[512,768]{1,0:T(8,128)(2,1)S(1)}, u32[]{:S(2)}) copy-start(bf16[512,768]{1,0:T(8,128)(2,1)S(1)} %get-tuple-element.372) | copy-start | bytes 2359300
  345.7 12.7 %copy-start.41 = (f32[512]{0:T(512)}, f32[512]{0:T(512)S(1)}, u32[]{:S(2)}) copy-start(f32[512]{0:T(512)S(1)} %negate_multiply_fusion.1) | copy-start | bytes 6148
  350.5 15.9 %all-to-all-start.4 = ((bf16[512,4,192]{0,2,1:T(8,128)(2,1)}), bf16[512,4,192]{0,2,1:T(8,128)(2,1)}, u32[]{:S(2)}, u32[]{:S(2)}) async-start(bf16[512,4,192]{0,2,1:T(8,128)(2,1)} %bitcast.25), calls=%async_computation.4 | async-start | bytes 1572864 | tf_op jit(solution)/shard_map/all_to_all | solution.py:199
  354.7 244.3 %reduce-scatter.7.cloned.1.call-start = ((), (), s32[]{:S(2)}) async-start(), calls=%async_computation.17 | async-start | bytes 2654208 | tf_op jit(solution)/shard_map/reduce_scatter | solution.py:280
  354.8 18.0 %copy-start.5 = (bf16[2048,3,64]{0,2,1:T(8,128)(2,1)S(1)}, bf16[2048,3,64]{0,2,1:T(8,128)(2,1)}, u32[]{:S(2)}) copy-start(bf16[2048,3,64]{0,2,1:T(8,128)(2,1)} %copy-done.4) | copy-start | bytes 2359300
  490.1 29.3 %copy-start.15 = (bf16[4,512,3,64]{1,3,2,0:T(8,128)(2,1)S(1)}, bf16[4,512,3,64]{1,3,2,0:T(8,128)(2,1)}, u32[]{:S(2)}) copy-start(bf16[4,512,3,64]{1,3,2,0:T(8,128)(2,1)} %get-tuple-element.132) | copy-start | bytes 2359300
  490.1 15.3 %all-to-all-start.6 = ((bf16[4,512,192]{1,2,0:T(8,128)(2,1)}), bf16[4,512,192]{1,2,0:T(8,128)(2,1)S(1)}, u32[]{:S(2)}, u32[]{:S(2)}) async-start(bf16[4,512,192]{1,2,0:T(8,128)(2,1)} %copy.92), calls=%async_computation.6 | async-start | bytes 1572864 | tf_op jit(solution)/shard_map/all_to_all | solution.py:242
  493.7 174.0 %reduce-scatter.5.cloned.1.call-start = ((), (), s32[]{:S(2)}) async-start(), calls=%async_computation.16 | async-start | bytes 7962624 | tf_op jit(solution)/shard_map/reduce_scatter | solution.py:278
  505.3 14.1 %copy-start.18 = (bf16[4,512,192]{1,2,0:T(8,128)(2,1)}, bf16[4,512,192]{1,2,0:T(8,128)(2,1)S(1)}, u32[]{:S(2)}) copy-start(bf16[4,512,192]{1,2,0:T(8,128)(2,1)S(1)} %all-to-all-done.6) | copy-start | bytes 2359300
  540.1 294.1 %reduce-scatter.11.cloned.1.call-start = ((), (), s32[]{:S(2)}) async-start(), calls=%async_computation.19 | async-start | bytes 10616832 | tf_op jit(solution)/shard_map/reduce_scatter | solution.py:286
  549.4 451.2 %reduce-scatter.9.cloned.1.call-start = ((), (), s32[]{:S(2)}) async-start(), calls=%async_computation.18 | async-start | bytes 10616832 | tf_op jit(solution)/shard_map/reduce_scatter | solution.py:284
  558.1 444.7 %copy-start.11 = (f32[512,768]{1,0:T(8,128)S(1)}, f32[512,768]{1,0:T(8,128)}, u32[]{:S(2)}) copy-start(f32[512,768]{1,0:T(8,128)} %copy-done.10) | copy-start | bytes 4718596
  558.1 444.7 %copy-start.42 = (f32[512]{0:T(512)S(1)}, f32[512]{0:T(512)}, u32[]{:S(2)}) copy-start(f32[512]{0:T(512)} %copy-done.41) | copy-start | bytes 6148
  558.1 444.7 %copy-start.52 = (pred[512]{0:T(512)(128)(4,1)S(1)}, pred[512]{0:T(512)(128)(4,1)}, u32[]{:S(2)}) copy-start(pred[512]{0:T(512)(128)(4,1)} %copy-done.51) | copy-start | bytes 1540
  558.1 493.3 %all-reduce.21.cloned.1.call-start = ((), (), s32[]{:S(2)}) async-start(), calls=%async_computation.20 | async-start | bytes 3538944 | tf_op jit(solution)/shard_map/psum | solution.py:307
  1002.9 55.6 %copy-start.1 = (bf16[1,10,768]{2,1,0:T(8,128)(2,1)S(1)}, bf16[1,10,768]{2,1,0:T(8,128)(2,1)}, u32[]{:S(2)}) copy-start(bf16[1,10,768]{2,1,0:T(8,128)(2,1)} %param.22) | copy-start | bytes 46084
  (37 other events, 164.6 us)
Sparse Core Ops, SparseCore 0:
  10.2 81.7 all-gather.5
  94.2 59.5 all-gather.7
  156.0 92.1 all-gather.9
  250.2 78.1 all-gather.11
  358.8 67.5 reduce-scatter.6
  540.2 127.5 reduce-scatter.4
  671.8 162.3 reduce-scatter.10
  838.2 162.3 reduce-scatter.8
  1004.6 46.7 all-reduce.20
